TPU v7x, 32 devices: a whole 2x2x4 slice. The times are simulated.
32 devices in a mesh: pts: 8 (over y, x, core), cen: 4 (over z).
Axes of the slice: x: 2, y: 2, z: 4, core: 2. Of those that a mesh axis runs over, the one named last changes fastest.
Arguments:
- embeddings: float32 [8192, 64], P('pts'), may hold values from -0.75 to 0.75
- centroids: float32 [8192, 64], P('cen'), may hold values from -0.75 to 0.75
- point_duals: float32 [8192], P('pts'), may hold values from -4 to 0.1
- centroid_duals: float32 [8192], P('cen'), may hold values from -1.5 to 2.6
- targets: float32 [8192, 64], P('pts'), may hold values from -6 to 6
Outputs:
- grad_emb: float32 [8192, 64], P('pts')
- grad_cen: float32 [8192, 64], P(('cen', 'pts'))
All inputs are finite; a program needn't handle non-finite values.
Results may differ from a plain program's by a relative error of at most 0.0003.
Values sent between devices are 32-bit elements; how exact they have to be, the bound alone decides.
No kernel may reach another device: no remote copies, remote signals or barrier semaphores. Data moves between devices by JAX's collectives and lax.ppermute only.
A program may use at most 64 MiB of HBM per device.

v0:
```python
import jax
import jax.numpy as jnp
from jax import lax
from jax.sharding import PartitionSpec as P

ITERS = 3
EPSILON = 0.08


def plan_block(points, duals_row, cen_block, duals_block, plan_total):
    scores = jnp.dot(
        points, cen_block.T, precision=lax.Precision.HIGHEST, preferred_element_type=jnp.float32
    )
    return jnp.exp(duals_row[:, None] + duals_block[None, :] + scores / EPSILON) / plan_total


def shards(embeddings, centroids, point_duals, centroid_duals, targets):
    exact_mode = lax.Precision.HIGHEST
    cen_rows, feat_width = centroids.shape
    plan_total = float(cen_rows * lax.axis_size("cen"))
    block_cols = min(256, cen_rows)
    block_count = cen_rows // block_cols
    cen_blocks = centroids.reshape(block_count, block_cols, feat_width)
    dual_blocks = centroid_duals.reshape(block_count, block_cols)
    rows_zero = jnp.zeros(point_duals.shape, jnp.float32)

    def first_step(running, inputs):
        cen_block, duals_block = inputs
        plan_tile = plan_block(embeddings, point_duals, cen_block, duals_block, plan_total)
        target_scores = jnp.dot(
            targets, cen_block.T, precision=exact_mode, preferred_element_type=jnp.float32
        )
        weighted = plan_tile * target_scores
        return (
            (running[0] + plan_tile.sum(1), running[1] + weighted.sum(1)),
            (plan_tile.sum(0), weighted.sum(0)),
        )

    (row_mass, row_load), (col_mass, col_load) = lax.scan(
        first_step, (rows_zero, rows_zero), (cen_blocks, dual_blocks)
    )
    col_mass = col_mass.reshape(-1)
    col_load = col_load.reshape(-1)
    row_mass, row_load = lax.psum((row_mass, row_load), "cen")
    col_mass, col_load = lax.psum((col_mass, col_load), "pts")
    col_scale = col_load / col_mass
    row_scale = row_load / row_mass
    for sweep_turn in range(ITERS):
        adjoint_scale_blocks = col_scale.reshape(block_count, block_cols)

        def sweep_step(running, inputs):
            cen_block, duals_block, scale_block = inputs
            plan_tile = plan_block(embeddings, point_duals, cen_block, duals_block, plan_total)
            row_part = jnp.dot(
                plan_tile, scale_block, precision=exact_mode, preferred_element_type=jnp.float32
            )
            col_part = jnp.dot(
                row_scale, plan_tile, precision=exact_mode, preferred_element_type=jnp.float32
            )
            return (running + row_part, col_part)

        row_terms, col_terms = lax.scan(
            sweep_step, rows_zero, (cen_blocks, dual_blocks, adjoint_scale_blocks)
        )
        row_terms, col_terms = (row_terms, col_terms.reshape(-1))
        row_terms = lax.psum(row_terms, "cen")
        col_terms = lax.psum(col_terms, "pts")
        col_scale = (col_load - col_terms) / col_mass
        row_scale = (row_load - row_terms) / row_mass
    scale_blocks = col_scale.reshape(block_count, block_cols)
    emb_zero = jnp.zeros((embeddings.shape[0], feat_width), jnp.float32)

    def block_weights(cen_block, duals_block, scale_block):
        plan_tile = plan_block(embeddings, point_duals, cen_block, duals_block, plan_total)
        target_scores = jnp.dot(
            targets, cen_block.T, precision=exact_mode, preferred_element_type=jnp.float32
        )
        return plan_tile * (target_scores - row_scale[:, None] - scale_block[None, :])

    def final_step(running, inputs):
        cen_block, duals_block, scale_block = inputs
        weights = block_weights(cen_block, duals_block, scale_block)
        emb_part = jnp.dot(
            weights, cen_block, precision=exact_mode, preferred_element_type=jnp.float32
        )
        cen_part = lax.dot_general(
            weights,
            embeddings,
            (((0,), (0,)), ((), ())),
            precision=exact_mode,
            preferred_element_type=jnp.float32,
        )
        return (running + emb_part, cen_part)

    emb_local, cen_parts = lax.scan(final_step, emb_zero, (cen_blocks, dual_blocks, scale_blocks))
    grad_cen = lax.psum_scatter(
        cen_parts.reshape(cen_rows, feat_width), "pts", scatter_dimension=0, tiled=True
    )
    grad_emb = lax.psum(emb_local, "cen")
    return (grad_emb, grad_cen)


def solution(mesh):
    in_specs = (P("pts", None), P("cen", None), P("pts"), P("cen"), P("pts", None))
    out_specs = (P("pts", None), P(("cen", "pts"), None))
    return jax.shard_map(shards, mesh=mesh, in_specs=in_specs, out_specs=out_specs, check_vma=False)
```

profile of v0, /device:TPU:0, one launch (start us, length us, event | category | flops | bytes accessed | tf_op | source)
XLA Modules:
  0.0 287.0 jit_solution(17219121614646234759)
XLA Ops:
  8.8 1.4 copy.7
  10.9 20.4 %while.69 = (s32[]{:T(128)}, f32[1024]{0:T(1024)S(1)}, f32[1024]{0:T(1024)S(1)}, f32[8,256]{1,0:T(8,128)S(1)}, f32[8,256]{1,0:T(8,128)S(1)}, /*index=5*/f32[1024...) while((s32[]{:T(128)}, f32[1024]{0:T(1024)S(1)}, ...), condition=%wide.region_5.6_spmd.clone, body=%wide.region_0.5_spmd.clone.sunk | while | flops 405014016 | bytes 2929819 | solution.py:39
  10.9 1.3 fusion.127
  13.5 1.3 fusion.127
  14.8 1.1 fusion.128
  16.0 1.3 fusion.127
  17.3 1.1 fusion.128
  18.6 1.3 fusion.127
  19.9 1.1 fusion.128
  21.1 1.3 fusion.127
  22.4 1.1 fusion.128
  23.7 1.3 fusion.127
  25.0 1.1 fusion.128
  26.2 1.3 fusion.127
  27.5 1.1 fusion.128
  28.8 1.3 fusion.127
  30.1 1.1 fusion.128
  31.3 25.5 %all-reduce = (f32[2048]{0:T(1024)S(1)}, f32[2048]{0:T(1024)S(1)}) all-reduce(f32[2048]{0:T(1024)S(1)} %bitcast.258, f32[2048]{0:T(1024)S(1)} %bitcast.259), channel_id=1, replica_groups=mesh['pts'=8,'cen'=4] {'pts'}, use_global_device_ids=true, to_apply=%region_7.8 | all-reduce | flops 4096 | bytes 32768 | tf_op jit(solution)/shard_map/psum | solution.py:45
  56.9 12.1 %all-reduce.1 = (f32[1024]{0:T(1024)S(1)}, f32[1024]{0:T(1024)S(1)}) all-reduce(f32[1024]{0:T(1024)S(1)} %get-tuple-element.257, f32[1024]{0:T(1024)S(1)} %get-tuple-element.254), channel_id=1, replica_groups=mesh['pts'=8,'cen'=4] {'cen'}, use_global_device_ids=true, to_apply=%region_9.10 | all-reduce | flops 2048 | bytes 16384 | tf_op jit(solution)/shard_map/psum | solution.py:44
  69.0 22.4 %while.70 = (s32[]{:T(128)}, f32[1024]{0:T(1024)S(1)}, f32[8,256]{1,0:T(8,128)S(1)}, f32[1024]{0:T(1024)S(1)}, f32[8,256]{1,0:T(8,128)S(1)}, /*index=5*/f32[8,25...) while((s32[]{:T(128)}, f32[1024]{0:T(1024)S(1)}, ...), condition=%wide.region_11.12_spmd.clone, body=%wide.region_10.11_spmd.clone.sunk | while | flops 208668672 | bytes 3570831 | solution.py:62
  69.1 1.1 fusion.135
  71.9 1.1 fusion.135
  74.7 1.1 fusion.135
  77.5 1.1 fusion.135
  80.3 1.1 fusion.135
  83.1 1.1 fusion.135
  85.9 1.1 fusion.135
  88.7 1.1 fusion.135
  91.5 12.1 %psum.81 = f32[2048]{0:T(1024)S(1)} all-reduce(f32[2048]{0:T(1024)S(1)} %bitcast.260), channel_id=1, replica_groups=mesh['pts'=8,'cen'=4] {'pts'}, use_global_device_ids=true, to_apply=%region_12.13 | all-reduce | flops 2048 | bytes 16384 | tf_op jit(solution)/shard_map/psum | solution.py:67
  103.6 8.4 %psum.82 = f32[1024]{0:T(1024)S(1)} all-reduce(f32[1024]{0:T(1024)S(1)} %get-tuple-element.259), channel_id=1, replica_groups=mesh['pts'=8,'cen'=4] {'cen'}, use_global_device_ids=true, to_apply=%region_13.14 | all-reduce | flops 1024 | bytes 8192 | tf_op jit(solution)/shard_map/psum | solution.py:66
  112.0 22.4 %while.71 = (s32[]{:T(128)}, f32[1024]{0:T(1024)S(1)}, f32[8,256]{1,0:T(8,128)S(1)}, f32[1024]{0:T(1024)S(1)}, f32[8,256]{1,0:T(8,128)S(1)}, /*index=5*/f32[8,25...) while((s32[]{:T(128)}, f32[1024]{0:T(1024)S(1)}, ...), condition=%wide.region_15.16_spmd.clone, body=%wide.region_14.15_spmd.clone.sunk | while | flops 208668672 | bytes 3570831 | solution.py:62
  112.1 1.1 fusion.144
  114.9 1.1 fusion.144
  117.7 1.1 fusion.144
  120.5 1.1 fusion.144
  123.3 1.1 fusion.144
  126.1 1.1 fusion.144
  128.9 1.1 fusion.144
  131.7 1.1 fusion.144
  134.5 12.1 %psum.83 = f32[2048]{0:T(1024)S(1)} all-reduce(f32[2048]{0:T(1024)S(1)} %bitcast.261), channel_id=1, replica_groups=mesh['pts'=8,'cen'=4] {'pts'}, use_global_device_ids=true, to_apply=%region_16.17 | all-reduce | flops 2048 | bytes 16384 | tf_op jit(solution)/shard_map/psum | solution.py:67
  146.6 10.4 %psum.84 = f32[1024]{0:T(1024)S(1)} all-reduce(f32[1024]{0:T(1024)S(1)} %get-tuple-element.261), channel_id=1, replica_groups=mesh['pts'=8,'cen'=4] {'cen'}, use_global_device_ids=true, to_apply=%region_17.18 | all-reduce | flops 1024 | bytes 8192 | tf_op jit(solution)/shard_map/psum | solution.py:66
  157.0 22.4 %while.72 = (s32[]{:T(128)}, f32[1024]{0:T(1024)S(1)}, f32[8,256]{1,0:T(8,128)S(1)}, f32[1024]{0:T(1024)S(1)}, f32[8,256]{1,0:T(8,128)S(1)}, /*index=5*/f32[8,25...) while((s32[]{:T(128)}, f32[1024]{0:T(1024)S(1)}, ...), condition=%wide.region_19.20_spmd.clone, body=%wide.region_18.19_spmd.clone.sunk | while | flops 208668672 | bytes 3570831 | solution.py:62
  157.0 1.1 fusion.153
  159.9 1.1 fusion.153
  162.7 1.1 fusion.153
  165.5 1.1 fusion.153
  168.3 1.1 fusion.153
  171.1 1.1 fusion.153
  173.9 1.1 fusion.153
  176.7 1.1 fusion.153
  179.5 8.4 %psum.85 = f32[1024]{0:T(1024)S(1)} all-reduce(f32[1024]{0:T(1024)S(1)} %get-tuple-element.262), channel_id=1, replica_groups=mesh['pts'=8,'cen'=4] {'cen'}, use_global_device_ids=true, to_apply=%region_21.22 | all-reduce | flops 1024 | bytes 8192 | tf_op jit(solution)/shard_map/psum | solution.py:66
  187.9 12.3 %psum.86 = f32[2048]{0:T(1024)S(1)} all-reduce(f32[2048]{0:T(1024)S(1)} %bitcast.262), channel_id=1, replica_groups=mesh['pts'=8,'cen'=4] {'pts'}, use_global_device_ids=true, to_apply=%region_20.21 | all-reduce | flops 2048 | bytes 16384 | tf_op jit(solution)/shard_map/psum | solution.py:67
  200.2 40.8 %while.73 = (s32[]{:T(128)}, f32[1024,64]{0,1:T(8,128)S(1)}, f32[8,256,64]{1,0,2:T(8,128)S(1)}, f32[1024]{0:T(1024)S(1)}, f32[8,256]{1,0:T(8,128)S(1)}, /*index=...) while((s32[]{:T(128)}, f32[1024,64]{0,1:T(8,128)S(1)}, ...), condition=%wide.region_23.24_spmd.clone, body=%wide.region_22.23_spmd.clone.sunk | while | flops 807272448 | bytes 7288987 | solution.py:95
  200.2 1.1 fusion.164
  205.3 1.1 fusion.164
  210.4 1.1 fusion.164
  215.5 1.1 fusion.164
  220.6 1.1 fusion.164
  225.7 1.1 fusion.164
  230.8 1.1 fusion.164
  235.9 1.1 fusion.164
  242.8 32.5 %all-reduce.4.cloned.1.call-done = f32[1024,64]{0,1:T(8,128)} async-done(((f32[1024,64]{0,1:T(8,128)}), f32[1024,64]{0,1:T(8,128)}) %all-reduce.4.cloned.1.call-update) | async-done | bytes 262160 | tf_op jit(solution)/shard_map/psum | solution.py:99
  275.3 2.5 reduce-scatter.2.cloned.1.call-done
  277.8 1.7 copy.77
  (246 shorter events, 75.6 us)
Async XLA Ops:
  8.0 267.3 %all-reduce.4.cloned.1.call-start = ((), (), s32[]{:S(2)}) async-start(), calls=%async_computation.1 | async-start | bytes 524288 | tf_op jit(solution)/shard_map/psum | solution.py:99
  8.1 0.7 copy-start.4
  8.8 1.5 copy-start
  8.8 1.5 copy-start.1
  10.2 0.7 copy-start.3
  241.0 0.7 copy-start.2
  241.8 36.1 %reduce-scatter.2.cloned.1.call-start = ((), (), s32[]{:S(2)}) async-start(), calls=%async_computation.2 | async-start | bytes 589824 | tf_op jit(solution)/shard_map/reduce_scatter | solution.py:96
Sparse Core Ops, SparseCore 0:
  241.9 33.3 all-reduce.3
Sparse Core Ops, SparseCore 1:
  245.9 31.9 reduce-scatter.1
where the time goes:
time: 287 us
  matrix products  117 us (41%)
  blocking collectives  101 us (35%)
  waiting for transfers between devices  35.1 us (12%)
  between operations  15.8 us (6%)
  local copies, waits for them, and re-layouts  15.5 us (5%)
    dot_general x40, matrix products, plan_block(): jnp.dot(points, cen_block.T, precision=lax.Precision.HIGHEST, preferred_e...  46.6 us
    psum x3, blocking collectives, shards(): col_terms = lax.psum(col_terms, 'pts')  36.5 us
    psum x1, waiting for transfers between devices, shards(): grad_emb = lax.psum(emb_local, 'cen')  32.5 us
    psum x3, blocking collectives, shards(): row_terms = lax.psum(row_terms, 'cen')  27.1 us
    psum x1, blocking collectives, shards(): col_mass, col_load = lax.psum((col_mass, col_load), 'pts')  25.5 us
    dot_general x24, matrix products, sweep_step(): jnp.dot(row_scale, plan_tile, precision=exact_mode, preferred_element_typ...  22 us
    dot_general x24, matrix products, sweep_step(): jnp.dot(plan_tile, scale_block, precision=exact_mode, preferred_element_t...  16.1 us
    psum x1, blocking collectives, shards(): row_mass, row_load = lax.psum((row_mass, row_load), 'cen')  12.1 us
  transfers between devices with their start and end apart: 2, of which 2 were waited for; matrix products, arithmetic and copies ran while one was open for 0% of the time, Pallas kernels for 0%

commit v1 on v0

--- a/solution.py
+++ b/solution.py
@@ -64,7 +64,7 @@
         )
         row_terms, col_terms = (row_terms, col_terms.reshape(-1))
         row_terms = lax.psum(row_terms, "cen")
-        col_terms = lax.psum(col_terms, "pts")
+        col_terms = jnp.sum(lax.all_gather(col_terms, "pts"), axis=0)
         col_scale = (col_load - col_terms) / col_mass
         row_scale = (row_load - row_terms) / row_mass
     scale_blocks = col_scale.reshape(block_count, block_cols)

time: 287 us -> 278 us (0.969)
  blocking collectives: 101 us -> 90.5 us
    psum x3 -> x0, blocking collectives: 36.5 us -> none  [shards(): col_terms = lax.psum(col_terms, 'pts')]
    all_gather x0 -> x3, blocking collectives: none -> 25.7 us  [shards(): col_terms = jnp.sum(lax.all_gather(col_terms, 'pts'), axis=0)]
where the time goes in v1:
time: 278 us; the launch traced here: 277 us
  matrix products  117 us (42%)
  blocking collectives  90.5 us (33%)
  waiting for transfers between devices  36 us (13%)
  between operations  15.7 us (6%)
  local copies, waits for them, and re-layouts  15.6 us (6%)
    dot_general x40, matrix products, plan_block(): jnp.dot(points, cen_block.T, precision=lax.Precision.HIGHEST, preferred_e...  46.6 us
    psum x1, waiting for transfers between devices, shards(): grad_emb = lax.psum(emb_local, 'cen')  33.5 us
    psum x3, blocking collectives, shards(): row_terms = lax.psum(row_terms, 'cen')  27.1 us
    all_gather x3, blocking collectives, shards(): col_terms = jnp.sum(lax.all_gather(col_terms, 'pts'), axis=0)  25.7 us
    psum x1, blocking collectives, shards(): col_mass, col_load = lax.psum((col_mass, col_load), 'pts')  25.5 us
    dot_general x24, matrix products, sweep_step(): jnp.dot(row_scale, plan_tile, precision=exact_mode, preferred_element_typ...  22 us
    dot_general x24, matrix products, sweep_step(): jnp.dot(plan_tile, scale_block, precision=exact_mode, preferred_element_t...  16.1 us
    psum x1, blocking collectives, shards(): row_mass, row_load = lax.psum((row_mass, row_load), 'cen')  12.1 us
  transfers between devices with their start and end apart: 2, of which 2 were waited for; matrix products, arithmetic and copies ran while one was open for 0% of the time, Pallas kernels for 0%

profile of v1, /device:TPU:0, one launch (start us, length us, event | category | flops | bytes accessed | tf_op | source)
XLA Modules:
  0.0 277.2 jit_solution(3084939179725667392)
XLA Ops:
  8.8 1.4 copy.9
  10.9 20.4 %while.69 = (s32[]{:T(128)}, f32[1024]{0:T(1024)S(1)}, f32[1024]{0:T(1024)S(1)}, f32[8,256]{1,0:T(8,128)S(1)}, f32[8,256]{1,0:T(8,128)S(1)}, /*index=5*/f32[1024...) while((s32[]{:T(128)}, f32[1024]{0:T(1024)S(1)}, ...), condition=%wide.region_5.6_spmd.clone, body=%wide.region_0.5_spmd.clone.sunk | while | flops 405014016 | bytes 2929819 | solution.py:39
  10.9 1.3 fusion.127
  13.5 1.3 fusion.127
  14.8 1.1 fusion.128
  16.0 1.3 fusion.127
  17.3 1.1 fusion.128
  18.6 1.3 fusion.127
  19.9 1.1 fusion.128
  21.1 1.3 fusion.127
  22.4 1.1 fusion.128
  23.7 1.3 fusion.127
  25.0 1.1 fusion.128
  26.2 1.3 fusion.127
  27.5 1.1 fusion.128
  28.8 1.3 fusion.127
  30.1 1.1 fusion.128
  31.3 25.5 %all-reduce = (f32[2048]{0:T(1024)S(1)}, f32[2048]{0:T(1024)S(1)}) all-reduce(f32[2048]{0:T(1024)S(1)} %bitcast.249, f32[2048]{0:T(1024)S(1)} %bitcast.250), channel_id=1, replica_groups=mesh['pts'=8,'cen'=4] {'pts'}, use_global_device_ids=true, to_apply=%region_7.8 | all-reduce | flops 4096 | bytes 32768 | tf_op jit(solution)/shard_map/psum | solution.py:45
  56.9 12.1 %all-reduce.1 = (f32[1024]{0:T(1024)S(1)}, f32[1024]{0:T(1024)S(1)}) all-reduce(f32[1024]{0:T(1024)S(1)} %get-tuple-element.257, f32[1024]{0:T(1024)S(1)} %get-tuple-element.254), channel_id=1, replica_groups=mesh['pts'=8,'cen'=4] {'cen'}, use_global_device_ids=true, to_apply=%region_9.10 | all-reduce | flops 2048 | bytes 16384 | tf_op jit(solution)/shard_map/psum | solution.py:44
  69.0 22.4 %while.70 = (s32[]{:T(128)}, f32[1024]{0:T(1024)S(1)}, f32[8,256]{1,0:T(8,128)S(1)}, f32[1024]{0:T(1024)S(1)}, f32[8,256]{1,0:T(8,128)S(1)}, /*index=5*/f32[8,25...) while((s32[]{:T(128)}, f32[1024]{0:T(1024)S(1)}, ...), condition=%wide.region_11.12_spmd.clone, body=%wide.region_10.11_spmd.clone.sunk | while | flops 208668672 | bytes 3570831 | solution.py:62
  69.1 1.1 fusion.135
  71.9 1.1 fusion.135
  74.7 1.1 fusion.135
  77.5 1.1 fusion.135
  80.3 1.1 fusion.135
  83.1 1.1 fusion.135
  85.9 1.1 fusion.135
  88.7 1.1 fusion.135
  91.5 8.2 %all-gather = f32[8,1,2048]{2,1,0:T(1,128)S(1)} all-gather(f32[1,1,2048]{2,1,0:T(1,128)S(1)} %reshape.46), channel_id=1, replica_groups=mesh['pts'=8,'cen'=4] {'pts'}, dimensions={0}, use_global_device_ids=true | all-gather | bytes 73728 | tf_op jit(solution)/shard_map/all_gather | solution.py:67
  99.8 8.4 %psum.60 = f32[1024]{0:T(1024)S(1)} all-reduce(f32[1024]{0:T(1024)S(1)} %get-tuple-element.259), channel_id=1, replica_groups=mesh['pts'=8,'cen'=4] {'cen'}, use_global_device_ids=true, to_apply=%region_13.14 | all-reduce | flops 1024 | bytes 8192 | tf_op jit(solution)/shard_map/psum | solution.py:66
  108.2 22.4 %while.71 = (s32[]{:T(128)}, f32[1024]{0:T(1024)S(1)}, f32[8,256]{1,0:T(8,128)S(1)}, f32[1024]{0:T(1024)S(1)}, f32[8,256]{1,0:T(8,128)S(1)}, /*index=5*/f32[8,25...) while((s32[]{:T(128)}, f32[1024]{0:T(1024)S(1)}, ...), condition=%wide.region_15.16_spmd.clone, body=%wide.region_14.15_spmd.clone.sunk | while | flops 208668672 | bytes 3570831 | solution.py:62
  108.2 1.1 fusion.144
  111.0 1.1 fusion.144
  113.8 1.1 fusion.144
  116.6 1.1 fusion.144
  119.4 1.1 fusion.144
  122.2 1.1 fusion.144
  125.0 1.1 fusion.144
  127.8 1.1 fusion.144
  130.6 9.3 %all-gather.1 = f32[8,1,2048]{2,1,0:T(1,128)S(1)} all-gather(f32[1,1,2048]{2,1,0:T(1,128)S(1)} %reshape.48), channel_id=1, replica_groups=mesh['pts'=8,'cen'=4] {'pts'}, dimensions={0}, use_global_device_ids=true | all-gather | bytes 73728 | tf_op jit(solution)/shard_map/all_gather | solution.py:67
  140.0 10.4 %psum.61 = f32[1024]{0:T(1024)S(1)} all-reduce(f32[1024]{0:T(1024)S(1)} %get-tuple-element.261), channel_id=1, replica_groups=mesh['pts'=8,'cen'=4] {'cen'}, use_global_device_ids=true, to_apply=%region_17.18 | all-reduce | flops 1024 | bytes 8192 | tf_op jit(solution)/shard_map/psum | solution.py:66
  150.4 22.4 %while.72 = (s32[]{:T(128)}, f32[1024]{0:T(1024)S(1)}, f32[8,256]{1,0:T(8,128)S(1)}, f32[1024]{0:T(1024)S(1)}, f32[8,256]{1,0:T(8,128)S(1)}, /*index=5*/f32[8,25...) while((s32[]{:T(128)}, f32[1024]{0:T(1024)S(1)}, ...), condition=%wide.region_19.20_spmd.clone, body=%wide.region_18.19_spmd.clone.sunk | while | flops 208668672 | bytes 3570831 | solution.py:62
  150.4 1.1 fusion.153
  153.2 1.1 fusion.153
  156.0 1.1 fusion.153
  158.8 1.1 fusion.153
  161.6 1.1 fusion.153
  164.4 1.1 fusion.153
  167.2 1.1 fusion.153
  170.0 1.1 fusion.153
  172.8 8.4 %psum.62 = f32[1024]{0:T(1024)S(1)} all-reduce(f32[1024]{0:T(1024)S(1)} %get-tuple-element.262), channel_id=1, replica_groups=mesh['pts'=8,'cen'=4] {'cen'}, use_global_device_ids=true, to_apply=%region_21.22 | all-reduce | flops 1024 | bytes 8192 | tf_op jit(solution)/shard_map/psum | solution.py:66
  181.2 8.2 %all-gather.2 = f32[8,1,2048]{2,1,0:T(1,128)S(1)} all-gather(f32[1,1,2048]{2,1,0:T(1,128)S(1)} %reshape.50), channel_id=1, replica_groups=mesh['pts'=8,'cen'=4] {'pts'}, dimensions={0}, use_global_device_ids=true | all-gather | bytes 73728 | tf_op jit(solution)/shard_map/all_gather | solution.py:67
  189.6 40.9 %while.73 = (s32[]{:T(128)}, f32[1024,64]{0,1:T(8,128)S(1)}, f32[8,256,64]{1,0,2:T(8,128)S(1)}, f32[1024]{0:T(1024)S(1)}, f32[8,256]{1,0:T(8,128)S(1)}, /*index=...) while((s32[]{:T(128)}, f32[1024,64]{0,1:T(8,128)S(1)}, ...), condition=%wide.region_23.24_spmd.clone, body=%wide.region_22.23_spmd.clone.sunk | while | flops 807272448 | bytes 7288987 | solution.py:95
  189.6 1.1 fusion.164
  194.7 1.1 fusion.164
  199.8 1.1 fusion.164
  204.9 1.1 fusion.164
  210.0 1.1 fusion.164
  215.1 1.1 fusion.164
  220.2 1.1 fusion.164
  225.3 1.1 fusion.164
  232.2 33.5 %all-reduce.4.cloned.1.call-done = f32[1024,64]{0,1:T(8,128)} async-done(((f32[1024,64]{0,1:T(8,128)}), f32[1024,64]{0,1:T(8,128)}) %all-reduce.4.cloned.1.call-update) | async-done | bytes 262160 | tf_op jit(solution)/shard_map/psum | solution.py:99
  265.6 2.5 reduce-scatter.2.cloned.1.call-done
  268.1 1.7 copy.82
  (249 shorter events, 75.8 us)
Async XLA Ops:
  8.0 257.6 %all-reduce.4.cloned.1.call-start = ((), (), s32[]{:S(2)}) async-start(), calls=%async_computation.1 | async-start | bytes 524288 | tf_op jit(solution)/shard_map/psum | solution.py:99
  8.1 0.7 copy-start.4
  8.8 1.5 copy-start
  8.8 1.5 copy-start.1
  10.2 0.7 copy-start.3
  230.4 0.7 copy-start.2
  231.1 37.0 %reduce-scatter.2.cloned.1.call-start = ((), (), s32[]{:S(2)}) async-start(), calls=%async_computation.2 | async-start | bytes 589824 | tf_op jit(solution)/shard_map/reduce_scatter | solution.py:96
Sparse Core Ops, SparseCore 0:
  231.3 34.3 all-reduce.3
Sparse Core Ops, SparseCore 1:
  235.3 32.8 reduce-scatter.1
